TPU v7x, 512 devices: a whole 4x8x8 slice. The times are simulated.
512 devices in a mesh: space: 64 (over y, x, z_hi), chan: 8 (over z_lo, core).
Axes of the slice: x: 4, y: 8, z: 8 (z_hi: 2, z_lo: 4; z = z_hi * 4 + z_lo), core: 2. Of those that a mesh axis runs over, the one named last changes fastest.
Arguments:
- source: bfloat16 [512, 192, 128], P('chan', 'space'), may hold values from -6 to 6
- kernel: bfloat16 [7, 7, 512, 512], P(None, None, 'chan'), may hold values from -0.0390625 to 0.0390625
Outputs:
- image: bfloat16 [512, 192, 128], P('chan', 'space')
All inputs are finite; a program needn't handle non-finite values.
Results may differ from a plain program's by a relative error of at most 0.001.
Values may be sent and summed in bfloat16 or wider, within the bound.
A program may use at most 64 MiB of HBM per device.

v0:
```python
import jax
import jax.numpy as jnp
from jax import lax
from jax.sharding import PartitionSpec as P

OFF = 7


def padded_2(array, sides, width):
    for axis, dim in sides:
        devices, length = (lax.axis_size(axis), array.shape[dim])
        up = [(i, (i + 1) % devices) for i in range(devices - 1)]
        down = [(j, i) for i, j in up]
        last = lax.slice_in_dim(array, length - width, length, axis=dim)
        initial = lax.slice_in_dim(array, 0, width, axis=dim)
        before = lax.ppermute(last, axis, up)
        after = lax.ppermute(initial, axis, down)
        array = jnp.concatenate([before, array, after], axis=dim)
    return array


def correlate(kernel, padded, height):
    reach = (OFF - 1) // 2
    width_cols = padded.shape[2]
    widened = jnp.pad(padded, ((0, 0), (0, 0), (reach, reach)))
    total = jnp.zeros((kernel.shape[2], height, width_cols), jnp.float32)
    for row_shift in range(OFF):
        window = widened[:, row_shift : row_shift + height, :]
        stacked = jnp.stack(
            [window[:, :, col_shift : col_shift + width_cols] for col_shift in range(OFF)]
        )
        weights = kernel[row_shift]
        total = total + jnp.einsum(
            "boc,bcxy->oxy", weights, stacked, preferred_element_type=jnp.float32
        )
    return total


def shards(source, kernel):
    reach = (OFF - 1) // 2
    height = source.shape[1]
    rimmed = padded_2(source, (("space", 1),), reach)
    coupled = correlate(kernel, lax.all_gather(rimmed, "chan", axis=0, tiled=True), height)
    return (source.astype(jnp.float32) - coupled).astype(jnp.bfloat16)


def solution(mesh):
    placed = (P("chan", "space", None), P(None, None, "chan", None))
    return jax.shard_map(
        shards, mesh=mesh, in_specs=placed, out_specs=P("chan", "space", None), check_vma=False
    )
```

profile of v0, /device:TPU:2, one launch (start us, length us, event | category | flops | bytes accessed | tf_op | source)
XLA Modules:
  0.0 92.9 jit_solution(15703168403566414398)
XLA Ops:
  6.5 10.9 %collective-permute-start = (bf16[64,3,128]{2,0,1:T(8,128)(2,1)}, bf16[64,3,128]{2,0,1:T(8,128)(2,1)S(1)}, u32[]{:S(2)}, u32[]{:S(2)}) collective-permute-start(bf16[64,3,128]{2,0,1:T(8,128)(2,1)} %param.2), channel_id=1, source_target_pairs={{0,8},{8,16},{16,24},{24,32},{32,40},{40,48},{48,56},{56,64},{64,7... | collective-permute-start | bytes 147464 | tf_op jit(solution)/shard_map/ppermute | solution.py:16
  17.5 1.9 %collective-permute-start.1 = (bf16[64,3,128]{2,0,1:T(8,128)(2,1)}, bf16[64,3,128]{2,0,1:T(8,128)(2,1)S(1)}, u32[]{:S(2)}, u32[]{:S(2)}) collective-permute-start(bf16[64,3,128]{2,0,1:T(8,128)(2,1)} %param.2), channel_id=1, source_target_pairs={{8,0},{16,8},{24,16},{32,24},{40,32},{48,40},{56,48},{64,56},{72,6... | collective-permute-start | bytes 147464 | tf_op jit(solution)/shard_map/ppermute | solution.py:17
  19.4 1.1 %collective-permute-done = bf16[64,3,128]{2,0,1:T(8,128)(2,1)S(1)} collective-permute-done((bf16[64,3,128]{2,0,1:T(8,128)(2,1)}, bf16[64,3,128]{2,0,1:T(8,128)(2,1)S(1)}, u32[]{:S(2)}, u32[]{:S(2)}) %collective-permute-start) | collective-permute-done | bytes 49184 | tf_op jit(solution)/shard_map/ppermute | solution.py:16
  20.5 7.9 %collective-permute-done.1 = bf16[64,3,128]{2,0,1:T(8,128)(2,1)S(1)} collective-permute-done((bf16[64,3,128]{2,0,1:T(8,128)(2,1)}, bf16[64,3,128]{2,0,1:T(8,128)(2,1)S(1)}, u32[]{:S(2)}, u32[]{:S(2)}) %collective-permute-start.1) | collective-permute-done | bytes 49184 | tf_op jit(solution)/shard_map/ppermute | solution.py:17
  28.4 1.5 %pad_maximum_fusion = bf16[64,9,128]{2,0,1:T(8,128)(2,1)} fusion(bf16[64,3,128]{2,0,1:T(8,128)(2,1)S(1)} %collective-permute-done.1, bf16[64,3,128]{2,0,1:T(8,128)(2,1)} %param.2, bf16[64,3,128]{2,0,1:T(8,128)(2,1)S(1)} %collective-permute-done), kind=kLoop, calls=%fused_computation.170 | loop fusion | flops 147456 | bytes 294912 | tf_op jit(solution)/shard_map/concatenate | solution.py:18
  29.9 39.3 %all-gather.2.cloned.1.call-done = bf16[512,9,128]{2,0,1:T(8,128)(2,1)} async-done(((bf16[64,9,128]{2,0,1:T(8,128)(2,1)}), bf16[512,9,128]{2,0,1:T(8,128)(2,1)}) %all-gather.2.cloned.1.call-update) | async-done | bytes 1179664 | tf_op jit(solution)/shard_map/all_gather | solution.py:43
  69.2 1.3 %fusion.36 = bf16[7,512,3,128]{3,1,2,0:T(8,128)(2,1)S(1)} fusion(bf16[512,9,128]{2,0,1:T(8,128)(2,1)} %all-gather.2.cloned.1.call-done), kind=kLoop, calls=%fused_computation.85 | loop fusion | bytes 1572864
  70.5 1.2 %fusion.38 = bf16[7,512,3,128]{3,1,2,0:T(8,128)(2,1)S(1)} fusion(bf16[7,512,3,128]{3,1,2,0:T(8,128)(2,1)S(1)} %fusion.36, bf16[512,9,128]{2,0,1:T(8,128)(2,1)} %all-gather.2.cloned.1.call-done), kind=kLoop, calls=%fused_computation.87 | loop fusion | bytes 1572864
  71.7 0.2 fusion.40
  72.0 0.2 fusion.42
  72.5 0.8 fusion.46
  74.3 1.0 %fusion.58 = (bf16[7,512,3,128]{3,1,2,0:T(8,128)(2,1)S(1)}, bf16[7,512,3,128]{3,1,2,0:T(8,128)(2,1)S(1)}, bf16[7,512,3,128]{3,1,2,0:T(8,128)(2,1)S(1)}, bf16[7,5...) fusion(bf16[7,512,3,128]{3,1,2,0:T(8,128)(2,1)S(1)} %fusion.56, bf16[512,9,128]{2,0,1:T(8,128)(2,1)S(1)} %copy-done, ...), kind=kLoop, calls=%fused_computation.107 | loop fusion | bytes 3145728 | tf_op jit(solution)/shard_map/stack | solution.py:29
  76.0 0.8 fusion.70
  77.1 0.4 fusion.80
  77.5 0.6 fusion.82
  78.3 0.4 fusion.94
  79.0 1.0 %copy-done.1 = bf16[7,7,64,512]{3,2,1,0:T(8,128)(2,1)S(1)} copy-done((bf16[7,7,64,512]{3,2,1,0:T(8,128)(2,1)S(1)}, bf16[7,7,64,512]{3,2,1,0:T(8,128)(2,1)}, u32[]{:S(2)}) %copy-start.1) | copy-done | bytes 3211288
  80.0 0.6 convolution_bitcast_fusion
  80.6 0.6 convolution_bitcast_fusion.1
  81.1 0.6 convolution_bitcast_fusion.2
  81.7 0.6 convolution_bitcast_fusion.3
  82.3 0.6 convolution_bitcast_fusion.4
  82.8 0.6 convolution_bitcast_fusion.5
  84.8 1.2 %fusion.8 = bf16[64,3,128]{2,0,1:T(8,128)(2,1)} fusion(f32[3,128,64]{1,2,0:T(8,128)S(1)} %convolution_bitcast_fusion, f32[3,128,64]{1,2,0:T(8,128)S(1)} %convolution_bitcast_fusion.1, f32[3,128,64]{1,2,0:T(8,128)S(1)} %convolution_bitcast_fusion.2, f32[3,128,64]{1,2,0:T(8,128)S(1)} %convolution_bitcast_fusion.3, ...), kind=kOutput, calls=%fused_computation.57 | convolution fusion | flops 176381952 | bytes 3899392 | tf_op jit(solution)/shard_map/boc,bcxy->oxy/dot_general | solution.py:33
  (29 shorter events, 4.1 us)
Async XLA Ops:
  6.5 62.7 %all-gather.2.cloned.1.call-start = ((), (), s32[]{:S(2)}) async-start(), calls=%async_computation | async-start | bytes 1327104 | tf_op jit(solution)/shard_map/all_gather | solution.py:43
  6.5 13.9 %collective-permute-start = (bf16[64,3,128]{2,0,1:T(8,128)(2,1)}, bf16[64,3,128]{2,0,1:T(8,128)(2,1)S(1)}, u32[]{:S(2)}, u32[]{:S(2)}) collective-permute-start(bf16[64,3,128]{2,0,1:T(8,128)(2,1)} %param.2), channel_id=1, source_target_pairs={{0,8},{8,16},{16,24},{24,32},{32,40},{40,48},{48,56},{56,64},{64,7... | collective-permute-start | bytes 147464 | tf_op jit(solution)/shard_map/ppermute | solution.py:16
  17.5 11.0 %collective-permute-start.1 = (bf16[64,3,128]{2,0,1:T(8,128)(2,1)}, bf16[64,3,128]{2,0,1:T(8,128)(2,1)S(1)}, u32[]{:S(2)}, u32[]{:S(2)}) collective-permute-start(bf16[64,3,128]{2,0,1:T(8,128)(2,1)} %param.2), channel_id=1, source_target_pairs={{8,0},{16,8},{24,16},{32,24},{40,32},{48,40},{56,48},{64,56},{72,6... | collective-permute-start | bytes 147464 | tf_op jit(solution)/shard_map/ppermute | solution.py:17
  69.2 2.5 %copy-start = (bf16[512,9,128]{2,0,1:T(8,128)(2,1)S(1)}, bf16[512,9,128]{2,0,1:T(8,128)(2,1)}, u32[]{:S(2)}) copy-start(bf16[512,9,128]{2,0,1:T(8,128)(2,1)} %all-gather.2.cloned.1.call-done) | copy-start | bytes 3538948
  78.1 1.9 %copy-start.1 = (bf16[7,7,64,512]{3,2,1,0:T(8,128)(2,1)S(1)}, bf16[7,7,64,512]{3,2,1,0:T(8,128)(2,1)}, u32[]{:S(2)}) copy-start(bf16[7,7,64,512]{3,2,1,0:T(8,128)(2,1)} %param.3) | copy-start | bytes 9633796
  84.0 0.8 copy-start.2
Sparse Core Ops, SparseCore 0:
  30.0 39.1 all-gather.1
where the time goes:
time: 93.2 us; the launch traced here: 92.9 us
  waiting for transfers between devices  48.3 us (52%)
  between operations  13.6 us (15%)
  starting transfers between devices  12.8 us (14%)
  local copies, waits for them, and re-layouts  12 us (13%)
  matrix products  4.56 us (5%)
  other arithmetic  1.48 us (2%)
    all_gather x1, waiting for transfers between devices, shards(): lax.all_gather(rimmed, 'chan', axis=0, tiled=True)  39.3 us
    ppermute x1, starting transfers between devices, padded_2(): before = lax.ppermute(last, axis, up)  10.9 us
    unnamed x31, local copies, waits for them, and re-layouts  7.99 us
    ppermute x1, waiting for transfers between devices, padded_2(): after = lax.ppermute(initial, axis, down)  7.92 us
    dot_general x7, matrix products, correlate(): jnp.einsum('boc,bcxy->oxy', weights, stacked, preferred_element_type=jnp....  4.56 us
    another operation x7, local copies, waits for them, and re-layouts, correlate(): jnp.stack([window[:, :, col_shift:col_shift + width_cols] for col_shift i...  4.06 us
    ppermute x1, starting transfers between devices, padded_2(): after = lax.ppermute(initial, axis, down)  1.92 us
  transfers between devices with their start and end apart: 3, of which 3 were waited for; matrix products, arithmetic and copies ran while one was open for 0% of the time, Pallas kernels for 0%

commit v1 on v0

--- a/solution.py
+++ b/solution.py
@@ -40,7 +40,13 @@
     reach = (OFF - 1) // 2
     height = source.shape[1]
     rimmed = padded_2(source, (("space", 1),), reach)
-    coupled = correlate(kernel, lax.all_gather(rimmed, "chan", axis=0, tiled=True), height)
+    coupled = correlate(
+        kernel,
+        jnp.concatenate(
+            lax.all_to_all(jnp.stack([rimmed] * lax.axis_size("chan")), "chan", 0, 0), axis=0
+        ),
+        height,
+    )
     return (source.astype(jnp.float32) - coupled).astype(jnp.bfloat16)
 
 

time: 93.2 us -> 71.8 us (0.77)
  the two profiles are of different devices: /device:TPU:2 before, /device:TPU:1 now
where the time goes in v1:
time: 71.8 us; the launch traced here: 71.5 us
  blocking collectives  35.1 us (49%)
  starting transfers between devices  12.7 us (18%)
  local copies, waits for them, and re-layouts  10.3 us (14%)
  waiting for transfers between devices  7.71 us (11%)
  matrix products  4.57 us (6%)
  other arithmetic  0.82 us (1%)
    all_to_all x1, blocking collectives, shards(): lax.all_to_all(jnp.stack([rimmed] * lax.axis_size('chan')), 'chan', 0, 0)  35.1 us
    ppermute x1, starting transfers between devices, padded_2(): before = lax.ppermute(last, axis, up)  11.5 us
    ppermute x1, waiting for transfers between devices, padded_2(): after = lax.ppermute(initial, axis, down)  7.53 us
    unnamed x29, local copies, waits for them, and re-layouts  5.86 us
    dot_general x7, matrix products, correlate(): jnp.einsum('boc,bcxy->oxy', weights, stacked, preferred_element_type=jnp....  4.57 us
    another operation x7, local copies, waits for them, and re-layouts, correlate(): jnp.stack([window[:, :, col_shift:col_shift + width_cols] for col_shift i...  4.06 us
  transfers between devices with their start and end apart: 2, of which 2 were waited for; matrix products, arithmetic and copies ran while one was open for 0% of the time, Pallas kernels for 0%

profile of v1, /device:TPU:1, one launch (start us, length us, event | category | flops | bytes accessed | tf_op | source)
XLA Modules:
  0.0 71.5 jit_solution(2115531813992024407)
XLA Ops:
  0.0 11.5 %collective-permute-start = (bf16[64,3,128]{2,0,1:T(8,128)(2,1)}, bf16[64,3,128]{2,0,1:T(8,128)(2,1)S(1)}, u32[]{:S(2)}, u32[]{:S(2)}) collective-permute-start(bf16[64,3,128]{2,0,1:T(8,128)(2,1)} %param.2), channel_id=1, source_target_pairs={{0,8},{8,16},{16,24},{24,32},{32,40},{40,48},{48,56},{56,64},{64,7... | collective-permute-start | bytes 147464 | tf_op jit(solution)/shard_map/ppermute | solution.py:16
  11.5 1.3 %collective-permute-start.1 = (bf16[64,3,128]{2,0,1:T(8,128)(2,1)}, bf16[64,3,128]{2,0,1:T(8,128)(2,1)S(1)}, u32[]{:S(2)}, u32[]{:S(2)}) collective-permute-start(bf16[64,3,128]{2,0,1:T(8,128)(2,1)} %param.2), channel_id=1, source_target_pairs={{8,0},{16,8},{24,16},{32,24},{40,32},{48,40},{56,48},{64,56},{72,6... | collective-permute-start | bytes 147464 | tf_op jit(solution)/shard_map/ppermute | solution.py:17
  12.9 7.5 %collective-permute-done.1 = bf16[64,3,128]{2,0,1:T(8,128)(2,1)S(1)} collective-permute-done((bf16[64,3,128]{2,0,1:T(8,128)(2,1)}, bf16[64,3,128]{2,0,1:T(8,128)(2,1)S(1)}, u32[]{:S(2)}, u32[]{:S(2)}) %collective-permute-start.1) | collective-permute-done | bytes 49184 | tf_op jit(solution)/shard_map/ppermute | solution.py:17
  20.5 0.8 %pad_maximum_fusion = bf16[64,9,128]{2,0,1:T(8,128)(2,1)S(1)} fusion(bf16[64,3,128]{2,0,1:T(8,128)(2,1)S(1)} %collective-permute-done.1, bf16[64,3,128]{2,0,1:T(8,128)(2,1)} %param.2, bf16[64,3,128]{2,0,1:T(8,128)(2,1)S(1)} %collective-permute-done), kind=kLoop, calls=%fused_computation.170 | loop fusion | flops 147456 | bytes 294912 | tf_op jit(solution)/shard_map/concatenate | solution.py:18
  21.3 0.3 stack.179
  21.6 35.1 %all_to_all.5 = bf16[8,64,9,128]{3,1,2,0:T(8,128)(2,1)S(1)} all-to-all(bf16[8,64,9,128]{3,1,2,0:T(8,128)(2,1)S(1)} %stack.179), channel_id=1, replica_groups=mesh['space'=64,'chan'=8] {'chan'}, dimensions={0} | all-to-all | bytes 2359296 | tf_op jit(solution)/shard_map/all_to_all | solution.py:46
  57.1 0.2 fusion.38
  57.3 0.2 fusion.40
  57.6 0.2 fusion.42
  57.9 0.2 fusion.44
  58.1 0.8 %fusion.46 = (bf16[7,512,3,128]{3,1,2,0:T(8,128)(2,1)S(1)}, bf16[7,512,3,128]{3,1,2,0:T(8,128)(2,1)S(1)}, bf16[7,512,3,128]{3,1,2,0:T(8,128)(2,1)S(1)}, bf16[7,5...) fusion(bf16[7,512,3,128]{3,1,2,0:T(8,128)(2,1)S(1)} %fusion.44, ...), kind=kLoop, calls=%fused_computation.95 | loop fusion | bytes 3538944 | tf_op jit(solution)/shard_map/stack | solution.py:29
  59.9 1.0 %fusion.58 = (bf16[7,512,3,128]{3,1,2,0:T(8,128)(2,1)S(1)}, bf16[7,512,3,128]{3,1,2,0:T(8,128)(2,1)S(1)}, bf16[7,512,3,128]{3,1,2,0:T(8,128)(2,1)S(1)}, bf16[7,5...) fusion(bf16[7,512,3,128]{3,1,2,0:T(8,128)(2,1)S(1)} %fusion.56, bf16[512,9,128]{2,0,1:T(8,128)(2,1)S(1)} %bitcast.308, ...), kind=kLoop, calls=%fused_computation.107 | loop fusion | bytes 3145728 | tf_op jit(solution)/shard_map/stack | solution.py:29
  61.6 0.8 %fusion.70 = (bf16[7,512,3,128]{3,1,2,0:T(8,128)(2,1)S(1)}, bf16[7,512,3,128]{3,1,2,0:T(8,128)(2,1)S(1)}, bf16[7,512,3,128]{3,1,2,0:T(8,128)(2,1)S(1)}, bf16[7,512,3,128]{3,1,2,0:T(8,128)(2,1)S(1)}) fusion(bf16[7,512,3,128]{3,1,2,0:T(8,128)(2,1)S(1)} %fusion.68, bf16[512,9,128]{2,0,1:T(8,128)(2,1)S(1)} %bitcast.313, ...), kind=kLoop, calls=%fused_computation.119 | loop fusion | bytes 2752512 | tf_op jit(solution)/shard_map/stack | solution.py:29
  62.7 0.4 fusion.80
  63.1 0.6 fusion.82
  64.0 0.4 fusion.94
  64.6 1.0 %copy-done = bf16[7,7,64,512]{3,2,1,0:T(8,128)(2,1)S(1)} copy-done((bf16[7,7,64,512]{3,2,1,0:T(8,128)(2,1)S(1)}, bf16[7,7,64,512]{3,2,1,0:T(8,128)(2,1)}, u32[]{:S(2)}) %copy-start) | copy-done | bytes 3211288
  65.6 0.6 convolution_bitcast_fusion
  66.2 0.6 convolution_bitcast_fusion.1
  66.8 0.6 convolution_bitcast_fusion.2
  67.3 0.6 convolution_bitcast_fusion.3
  67.9 0.6 convolution_bitcast_fusion.4
  69.7 0.6 convolution_bitcast_fusion.5
  70.3 1.2 %fusion.8 = bf16[64,3,128]{2,0,1:T(8,128)(2,1)} fusion(f32[3,128,64]{1,2,0:T(8,128)S(1)} %convolution_bitcast_fusion, f32[3,128,64]{1,2,0:T(8,128)S(1)} %convolution_bitcast_fusion.1, f32[3,128,64]{1,2,0:T(8,128)S(1)} %convolution_bitcast_fusion.2, f32[3,128,64]{1,2,0:T(8,128)S(1)} %convolution_bitcast_fusion.3, ...), kind=kOutput, calls=%fused_computation.57 | convolution fusion | flops 176381952 | bytes 3899392 | tf_op jit(solution)/shard_map/boc,bcxy->oxy/dot_general | solution.py:33
  (27 shorter events, 4.3 us)
Async XLA Ops:
  0.0 12.9 %collective-permute-start = (bf16[64,3,128]{2,0,1:T(8,128)(2,1)}, bf16[64,3,128]{2,0,1:T(8,128)(2,1)S(1)}, u32[]{:S(2)}, u32[]{:S(2)}) collective-permute-start(bf16[64,3,128]{2,0,1:T(8,128)(2,1)} %param.2), channel_id=1, source_target_pairs={{0,8},{8,16},{16,24},{24,32},{32,40},{40,48},{48,56},{56,64},{64,7... | collective-permute-start | bytes 147464 | tf_op jit(solution)/shard_map/ppermute | solution.py:16
  11.5 9.0 %collective-permute-start.1 = (bf16[64,3,128]{2,0,1:T(8,128)(2,1)}, bf16[64,3,128]{2,0,1:T(8,128)(2,1)S(1)}, u32[]{:S(2)}, u32[]{:S(2)}) collective-permute-start(bf16[64,3,128]{2,0,1:T(8,128)(2,1)} %param.2), channel_id=1, source_target_pairs={{8,0},{16,8},{24,16},{32,24},{40,32},{48,40},{56,48},{64,56},{72,6... | collective-permute-start | bytes 147464 | tf_op jit(solution)/shard_map/ppermute | solution.py:17
  63.7 1.9 %copy-start = (bf16[7,7,64,512]{3,2,1,0:T(8,128)(2,1)S(1)}, bf16[7,7,64,512]{3,2,1,0:T(8,128)(2,1)}, u32[]{:S(2)}) copy-start(bf16[7,7,64,512]{3,2,1,0:T(8,128)(2,1)} %param.3) | copy-start | bytes 9633796
  69.5 0.8 %copy-start.1 = (bf16[64,3,128]{2,0,1:T(8,128)(2,1)S(1)}, bf16[64,3,128]{2,0,1:T(8,128)(2,1)}, u32[]{:S(2)}) copy-start(bf16[64,3,128]{2,0,1:T(8,128)(2,1)} %param.2) | copy-start | bytes 147460
